TPU v7x, 32 devices: a whole 2x2x4 slice. The times are simulated.
32 devices in a mesh: cells: 8 (over z, x), cent: 4 (over y, core).
Axes of the slice: x: 2, y: 2, z: 4, core: 2. Of those that a mesh axis runs over, the one named last changes fastest.
Arguments:
- embed: float32 [64, 32768], P(None, 'cells'), may hold values from -240 to 240
- centroids: float32 [64, 2048], P(None, 'cent'), may hold values from -8 to 8
- cell_weight: float32 [32768], P('cells'), may hold values from 0.5 to 18, as said below
Outputs:
- new_centroids: float32 [64, 2048], P(None, 'cent')
- log_norms: float32 [32768], P('cells')
Inputs may be any that keep to these rules, and one draw needn't show every extreme that they name: `cell_weight`: positive.
All inputs are finite; a program needn't handle non-finite values.
Results may differ from a plain program's by a relative error of at most 0.0003.
Values sent between devices are 32-bit elements; how exact they have to be, the bound alone decides.
A program may use at most 64 MiB of HBM per device.

v0:
```python
import jax
import jax.numpy as jnp
from jax import lax
from jax.sharding import PartitionSpec as P

ROW_BLOCK = 512
ROUNDS = 2


INV_TEMP = 0.125
PRIOR = 1.0


def block_logits(points, gathered, half_square):
    products = lax.dot_general(
        points, gathered, (((0,), (0,)), ((), ())), precision=lax.Precision.HIGHEST
    )
    return (products - half_square[None, :]) * INV_TEMP


def add_shares(points, shares, totals):
    moment = totals[0] + jnp.dot(points, shares, precision=lax.Precision.HIGHEST)
    masses = totals[1] + jnp.sum(shares, axis=0)
    return (moment, masses)


def accumulate(points, weights, logits, lognorm, totals):
    shares = jnp.exp(logits - lognorm[:, None]) * weights[:, None]
    return add_shares(points, shares, totals)


def on_device(embed, centroids, cell_weight):
    features, row_count = embed.shape
    own_rows = row_count // lax.axis_size("cent")
    offset = lax.axis_index("cent") * own_rows
    points_all = lax.dynamic_slice_in_dim(embed, offset, own_rows, 1)
    weights_all = lax.dynamic_slice_in_dim(cell_weight, offset, own_rows, 0)
    blocks = own_rows // ROW_BLOCK
    block_ids = jnp.arange(blocks, dtype=jnp.int32)
    current = centroids
    log_norms = None
    for round_id in range(ROUNDS):
        gathered = lax.all_gather(current, "cent", axis=1, tiled=True)
        half_square = 0.5 * jnp.sum(gathered * gathered, axis=0)
        initial = (
            jnp.zeros((features, gathered.shape[1]), jnp.float32),
            jnp.zeros((gathered.shape[1],), jnp.float32),
        )

        def pick_rows(block_id):
            start_row = block_id * ROW_BLOCK
            points = lax.dynamic_slice_in_dim(points_all, start_row, ROW_BLOCK, 1)
            weights = lax.dynamic_slice_in_dim(weights_all, start_row, ROW_BLOCK, 0)
            return (points, weights)

        def whole_block(totals, block_id):
            points, weights = pick_rows(block_id)
            logits = block_logits(points, gathered, half_square)
            peak = jnp.max(logits, axis=1)
            lognorm = peak + jnp.log(jnp.sum(jnp.exp(logits - peak[:, None]), axis=1))
            return (accumulate(points, weights, logits, lognorm, totals), lognorm)

        (moment, masses), norm_blocks = lax.scan(whole_block, initial, block_ids)
        log_norms = norm_blocks.reshape(own_rows)
        moment, masses = lax.psum((moment, masses), ("cells", "cent"))
        own_width = current.shape[1]
        first_col = lax.axis_index("cent") * own_width
        moment = lax.dynamic_slice_in_dim(moment, first_col, own_width, 1)
        masses = lax.dynamic_slice_in_dim(masses, first_col, own_width, 0)
        current = (moment + PRIOR * current) / (masses + PRIOR)[None, :]
    log_norms = lax.all_gather(log_norms, "cent", axis=0, tiled=True)
    return (current, log_norms)


def solution(mesh):
    in_specs = (P(None, "cells"), P(None, "cent"), P("cells"))
    out_specs = (P(None, "cent"), P("cells"))
    return jax.shard_map(
        on_device, mesh=mesh, in_specs=in_specs, out_specs=out_specs, check_vma=False
    )
```

profile of v0, /device:TPU:0, one launch (start us, length us, event | category | flops | bytes accessed | tf_op | source)
XLA Modules:
  0.0 349.3 jit_solution(84199073552617363)
XLA Ops:
  7.2 0.0 copy-start
  7.2 0.0 all-reduce.3.cloned.1.call-start
  7.3 1.1 copy-done
  8.4 0.7 dynamic_slice.38
  9.1 8.9 %all_gather.9 = f32[64,2048]{1,0:T(8,128)S(1)} all-gather(f32[64,512]{1,0:T(8,128)} %param.8), channel_id=1, replica_groups=mesh['cells'=8,'cent'=4] {'cent'}, dimensions={1}, use_global_device_ids=true | all-gather | bytes 655360 | tf_op jit(solution)/shard_map/all_gather | solution.py:43
  18.0 0.1 multiply_reduce_fusion.1
  18.1 0.0 copy-start.5
  18.1 26.7 %while.28 = (s32[]{:T(128)}, f32[64,2048]{1,0:T(8,128)S(1)}, f32[2048]{0:T(1024)S(1)}, s32[2]{0:T(128)S(1)}, f32[64,1024]{1,0:T(8,128)S(1)}, /*index=5*/f32[64,2...) while((s32[]{:T(128)}, f32[64,2048]{1,0:T(8,128)S(1)}, ...), condition=%wide.region_5.6_spmd.clone, body=%wide.region_1.5_spmd.clone.sunk | while | flops 1621362176 | bytes 35455200 | solution.py:63
  18.1 0.6 dynamic_slice.76
  19.3 3.8 %fusion.34 = (f32[512]{0:T(512)S(1)}, f32[512,2048]{1,0:T(8,128)S(1)}) fusion(f32[2048]{0:T(1024)S(1)} %get-tuple-element.336, f32[64,2048]{1,0:T(8,128)S(1)} %get-tuple-element.335, f32[64,1024]{1,0:T(8,128)S(1)} %get-tuple-element.334, s32[]{:T(128)S(6)} %select_n.24), kind=kOutput, calls=%fused_computation.37.clone.1 | convolution fusion | flops 808451584 | bytes 4859908 | tf_op jit(solution)/shard_map/while/body/eval_jaxpr/dot_general | solution.py:15
  23.1 0.0 copy-start.1
  23.2 0.7 exponential_reduce_fusion.4
  23.9 0.1 dynamic_slice.77
  23.9 1.1 copy-done.1
  25.1 0.8 fusion.36
  25.9 5.5 %fusion.35 = f32[64,2048]{1,0:T(8,128)S(1)} fusion(f32[512,2048]{1,0:T(8,128)} %copy-done.1, f32[512]{0:T(512)S(1)} %dynamic_slice.77, f32[512]{0:T(512)S(1)} %log_add_fusion.4, f32[64,2048]{1,0:T(8,128)S(1)} %get-tuple-element.319, pred[]{:T(512)S(6)} %compare.6, f32[64,1024]{1,0:T(8,128)S(1)} %get-tuple-element.334, s32[]{:T(128)S(6)} %select_n.24), kind=kOutput, calls=%fused_computation.5.clone.1 | convolution fusion | flops 807665664 | bytes 5378053 | tf_op jit(solution)/shard_map/while/body/eval_jaxpr/dot_general | solution.py:22
  31.4 0.6 dynamic_slice.76
  32.7 3.8 %fusion.34 = (f32[512]{0:T(512)S(1)}, f32[512,2048]{1,0:T(8,128)S(1)}) fusion(f32[2048]{0:T(1024)S(1)} %get-tuple-element.336, f32[64,2048]{1,0:T(8,128)S(1)} %get-tuple-element.335, f32[64,1024]{1,0:T(8,128)S(1)} %get-tuple-element.334, s32[]{:T(128)S(6)} %select_n.24), kind=kOutput, calls=%fused_computation.37.clone.1 | convolution fusion | flops 808451584 | bytes 4859908 | tf_op jit(solution)/shard_map/while/body/eval_jaxpr/dot_general | solution.py:15
  36.5 0.0 copy-start.1
  36.5 0.7 exponential_reduce_fusion.4
  37.2 0.1 dynamic_slice.77
  37.3 1.1 copy-done.1
  38.4 0.8 fusion.36
  39.3 5.5 %fusion.35 = f32[64,2048]{1,0:T(8,128)S(1)} fusion(f32[512,2048]{1,0:T(8,128)} %copy-done.1, f32[512]{0:T(512)S(1)} %dynamic_slice.77, f32[512]{0:T(512)S(1)} %log_add_fusion.4, f32[64,2048]{1,0:T(8,128)S(1)} %get-tuple-element.319, pred[]{:T(512)S(6)} %compare.6, f32[64,1024]{1,0:T(8,128)S(1)} %get-tuple-element.334, s32[]{:T(128)S(6)} %select_n.24), kind=kOutput, calls=%fused_computation.5.clone.1 | convolution fusion | flops 807665664 | bytes 5378053 | tf_op jit(solution)/shard_map/while/body/eval_jaxpr/dot_general | solution.py:22
  44.8 0.0 copy-start.4
  44.8 0.8 copy-done.4
  45.6 0.0 all-reduce.3.cloned.1.call-update
  45.6 0.0 all-reduce.5.cloned.1.call-start
  45.7 40.2 %psum.29 = f32[2048]{0:T(1024)S(1)} all-reduce(f32[2048]{0:T(1024)S(1)} %get-tuple-element.95), channel_id=1, replica_groups=mesh['cells'=8,'cent'=4] {'cells','cent'}, use_global_device_ids=true, to_apply=%region_7.8 | all-reduce | flops 2048 | bytes 16384 | tf_op jit(solution)/shard_map/psum | solution.py:65
  85.9 0.1 dynamic-slice_add_fusion.1
  86.0 89.9 %all-reduce.3.cloned.1.call-done = f32[64,2048]{1,0:T(8,128)} async-done(((f32[64,2048]{1,0:T(8,128)}), f32[64,2048]{1,0:T(8,128)}) %all-reduce.3.cloned.1.call-update) | async-done | bytes 524304 | tf_op jit(solution)/shard_map/psum | solution.py:65
  175.9 0.0 copy-done.5
  175.9 0.9 add_divide_fusion.1
  176.8 7.3 %all_gather.10 = f32[64,2048]{1,0:T(8,128)S(1)} all-gather(f32[64,512]{1,0:T(8,128)S(1)} %add_divide_fusion.1), channel_id=1, replica_groups=mesh['cells'=8,'cent'=4] {'cent'}, dimensions={1}, use_global_device_ids=true | all-gather | bytes 655360 | tf_op jit(solution)/shard_map/all_gather | solution.py:43
  184.2 0.1 multiply_reduce_fusion
  184.2 26.8 %while.29 = (s32[]{:T(128)}, f32[64,2048]{1,0:T(8,128)S(1)}, f32[2048]{0:T(1024)S(1)}, f32[2,512]{1,0:T(2,128)S(1)}, s32[2]{0:T(128)S(1)}, /*index=5*/f32[64,102...) while((s32[]{:T(128)}, f32[64,2048]{1,0:T(8,128)S(1)}, ...), condition=%wide.region_13.14_spmd.clone, body=%wide.region_9.13_spmd.clone.sunk | while | flops 1621362176 | bytes 35459308 | solution.py:63
  184.3 0.6 dynamic_slice.80
  185.5 3.8 %fusion.39 = (f32[512]{0:T(512)S(1)}, f32[512,2048]{1,0:T(8,128)S(1)}) fusion(f32[2048]{0:T(1024)S(1)} %get-tuple-element.375, f32[64,2048]{1,0:T(8,128)S(1)} %get-tuple-element.374, f32[64,1024]{1,0:T(8,128)S(1)} %get-tuple-element.373, s32[]{:T(128)S(6)} %select_n.25), kind=kOutput, calls=%fused_computation.38.clone.1 | convolution fusion | flops 808451584 | bytes 4859908 | tf_op jit(solution)/shard_map/while/body/eval_jaxpr/dot_general | solution.py:15
  189.3 0.0 copy-start.2
  189.3 0.7 exponential_reduce_fusion.5
  190.0 0.1 dynamic_slice.81
  190.1 1.1 copy-done.2
  191.2 0.8 fusion.41
  192.1 5.5 %fusion.40 = f32[64,2048]{1,0:T(8,128)S(1)} fusion(f32[512,2048]{1,0:T(8,128)} %copy-done.2, f32[512]{0:T(512)S(1)} %dynamic_slice.81, f32[512]{0:T(512)S(1)} %log_add_fusion.5, f32[64,2048]{1,0:T(8,128)S(1)} %get-tuple-element.356, pred[]{:T(512)S(6)} %compare.7, f32[64,1024]{1,0:T(8,128)S(1)} %get-tuple-element.373, s32[]{:T(128)S(6)} %select_n.25), kind=kOutput, calls=%fused_computation.19.clone.1 | convolution fusion | flops 807665664 | bytes 5378053 | tf_op jit(solution)/shard_map/while/body/eval_jaxpr/dot_general | solution.py:22
  197.7 0.6 dynamic_slice.80
  198.9 3.8 %fusion.39 = (f32[512]{0:T(512)S(1)}, f32[512,2048]{1,0:T(8,128)S(1)}) fusion(f32[2048]{0:T(1024)S(1)} %get-tuple-element.375, f32[64,2048]{1,0:T(8,128)S(1)} %get-tuple-element.374, f32[64,1024]{1,0:T(8,128)S(1)} %get-tuple-element.373, s32[]{:T(128)S(6)} %select_n.25), kind=kOutput, calls=%fused_computation.38.clone.1 | convolution fusion | flops 808451584 | bytes 4859908 | tf_op jit(solution)/shard_map/while/body/eval_jaxpr/dot_general | solution.py:15
  202.7 0.0 copy-start.2
  202.7 0.7 exponential_reduce_fusion.5
  203.4 0.1 dynamic_slice.81
  203.5 1.1 copy-done.2
  204.7 0.8 fusion.41
  205.5 5.5 %fusion.40 = f32[64,2048]{1,0:T(8,128)S(1)} fusion(f32[512,2048]{1,0:T(8,128)} %copy-done.2, f32[512]{0:T(512)S(1)} %dynamic_slice.81, f32[512]{0:T(512)S(1)} %log_add_fusion.5, f32[64,2048]{1,0:T(8,128)S(1)} %get-tuple-element.356, pred[]{:T(512)S(6)} %compare.7, f32[64,1024]{1,0:T(8,128)S(1)} %get-tuple-element.373, s32[]{:T(128)S(6)} %select_n.25), kind=kOutput, calls=%fused_computation.19.clone.1 | convolution fusion | flops 807665664 | bytes 5378053 | tf_op jit(solution)/shard_map/while/body/eval_jaxpr/dot_general | solution.py:22
  211.1 0.0 copy-start.3
  211.1 0.8 copy-done.3
  211.9 0.0 all-reduce.5.cloned.1.call-update
  211.9 5.2 %all_gather.11 = f32[4096]{0:T(1024)S(1)} all-gather(f32[1024]{0:T(1024)S(1)} %bitcast.18), channel_id=1, replica_groups=mesh['cells'=8,'cent'=4] {'cent'}, dimensions={0}, use_global_device_ids=true | all-gather | bytes 20480 | tf_op jit(solution)/shard_map/all_gather | solution.py:71
  217.1 39.2 %psum.31 = f32[2048]{0:T(1024)S(1)} all-reduce(f32[2048]{0:T(1024)S(1)} %get-tuple-element.97), channel_id=1, replica_groups=mesh['cells'=8,'cent'=4] {'cells','cent'}, use_global_device_ids=true, to_apply=%region_15.16 | all-reduce | flops 2048 | bytes 16384 | tf_op jit(solution)/shard_map/psum | solution.py:65
  256.3 0.1 dynamic-slice_add_fusion
  256.4 83.9 %all-reduce.5.cloned.1.call-done = f32[64,2048]{1,0:T(8,128)} async-done(((f32[64,2048]{1,0:T(8,128)}), f32[64,2048]{1,0:T(8,128)}) %all-reduce.5.cloned.1.call-update) | async-done | bytes 524304 | tf_op jit(solution)/shard_map/psum | solution.py:65
  340.2 1.6 add_divide_fusion
  341.8 0.6 copy.31
  (21 shorter events, 0.2 us)
Async XLA Ops:
  7.2 1.2 copy-start
  7.2 168.7 %all-reduce.3.cloned.1.call-start = ((), (), s32[]{:S(2)}) async-start(), calls=%async_computation | async-start | bytes 1048576 | tf_op jit(solution)/shard_map/psum | solution.py:65
  18.1 157.8 %copy-start.5 = (f32[64,512]{1,0:T(8,128)S(1)}, f32[64,512]{1,0:T(8,128)}, u32[]{:S(2)}) copy-start(f32[64,512]{1,0:T(8,128)} %param.8) | copy-start | bytes 393220
  23.1 1.9 copy-start.1
  36.5 1.9 copy-start.1
  44.8 0.8 copy-start.4
  45.6 294.6 %all-reduce.5.cloned.1.call-start = ((), (), s32[]{:S(2)}) async-start(), calls=%async_computation.1 | async-start | bytes 1048576 | tf_op jit(solution)/shard_map/psum | solution.py:65
  189.3 1.9 copy-start.2
  202.7 1.9 copy-start.2
  211.1 0.8 copy-start.3
Sparse Core Ops, SparseCore 0:
  45.8 130.0 all-reduce.2
  212.0 128.1 all-reduce.4
where the time goes:
time: 350 us; the launch traced here: 349 us
  waiting for transfers between devices  174 us (50%)
  blocking collectives  101 us (29%)
  matrix products  37.2 us (11%)
  between operations  14.2 us (4%)
  local copies, waits for them, and re-layouts  11.4 us (3%)
  other arithmetic  8.98 us (3%)
    psum x2, waiting for transfers between devices, on_device(): moment, masses = lax.psum((moment, masses), ('cells', 'cent'))  174 us
    psum x2, blocking collectives, on_device(): moment, masses = lax.psum((moment, masses), ('cells', 'cent'))  79.4 us
    dot_general x4, matrix products, add_shares(): jnp.dot(points, shares, precision=lax.Precision.HIGHEST)  22 us
    all_gather x2, blocking collectives, on_device(): gathered = lax.all_gather(current, 'cent', axis=1, tiled=True)  16.2 us
    dot_general x4, matrix products, block_logits(): lax.dot_general(points, gathered, (((0,), (0,)), ((), ())), precision=lax...  15.3 us
  transfers between devices with their start and end apart: 2, of which 2 were waited for; matrix products, arithmetic and copies ran while one was open for 0% of the time, Pallas kernels for 0%

commit v1 on v0

v1 whole, which is shorter than its diff:
```python
import functools

import jax
import jax.numpy as jnp
from jax import lax
from jax.experimental import pallas as pl
from jax.experimental.pallas import tpu as pltpu
from jax.sharding import PartitionSpec as P

ROUNDS = 2
INV_TEMP = 0.125
PRIOR = 1.0
TILE = 256
TILE2 = 1024
LANES = 128
MESH = pl.DeviceIdType.MESH
BF16 = jnp.bfloat16
F32 = jnp.float32


def split(x):
    high = x.astype(BF16)
    return high, x - high.astype(F32)


def kernel(
    n_cells, n_cent,
    embed_ref, cent_ref, weight_ref,
    out_ref, norm_ref,
    points, table, high, low, logits, peaks, sums, factor,
    current, partial, norms, parts,
    norm_send, norm_recv, part_send, part_recv, new_send, new_recv,
):
    features, cells = embed_ref.shape
    width = cent_ref.shape[1]
    rows = cells // LANES
    chunk = width // n_cells
    me_cells = lax.axis_index("cells")
    me_cent = lax.axis_index("cent")

    barrier = pltpu.get_barrier_semaphore()
    for d in range(1, n_cent):
        pl.semaphore_signal(
            barrier, inc=1, device_id={"cent": lax.rem(me_cent + d, n_cent)}, device_id_type=MESH
        )
    for d in range(1, n_cells):
        pl.semaphore_signal(
            barrier, inc=1, device_id={"cells": lax.rem(me_cells + d, n_cells)}, device_id_type=MESH
        )

    def stack_points(i, _):
        cols = pl.ds(pl.multiple_of(i * TILE, TILE), TILE)
        e1, rest = split(embed_ref[:, cols])
        e2, rest = split(rest)
        e3 = rest.astype(BF16)
        for j, term in enumerate((e1, e1, e2, e2, e1, e3)):
            points[j * features:(j + 1) * features, cols] = term
        points[6 * features:, cols] = jnp.ones((2 * features, TILE), BF16)
        return 0

    lax.fori_loop(0, cells // TILE, stack_points, 0)

    lane = lax.broadcasted_iota(jnp.int32, (width, LANES), 1)
    left = lane < features
    start = cent_ref[...].T
    current[0] = jnp.concatenate([start, start], axis=1)

    for r in range(ROUNDS):
        both = current[r]
        half_square = 0.5 * jnp.sum(jnp.where(left, both * both, 0.0), axis=1, keepdims=True)
        c1, rest = split(both * INV_TEMP)
        c2, rest = split(rest)
        c3 = rest
        h1, rest = split(jnp.broadcast_to(half_square * -INV_TEMP, (width, LANES)))
        h2, h3 = split(rest)
        c1, c2, h1, h2 = (x.astype(F32) for x in (c1, c2, h1, h2))
        first = jnp.where(left, c1, c2).astype(BF16)
        table[:, 0:LANES] = first
        table[:, LANES:2 * LANES] = first
        table[:, 2 * LANES:3 * LANES] = jnp.where(left, c3, c1).astype(BF16)
        table[:, 3 * LANES:] = jnp.where(
            lane == 0, h1, jnp.where(lane == 1, h2, jnp.where(lane == 2, h3, 0.0))
        ).astype(BF16)

        def score(i, _):
            cols = pl.ds(pl.multiple_of(i * TILE, TILE), TILE)
            logits[...] = jnp.dot(table[...], points[:, cols], preferred_element_type=F32)
            step = 64
            peak = logits[0:step, :]
            for k in range(step, width, step):
                peak = jnp.maximum(peak, logits[k:k + step, :])
            peak = jnp.max(peak, axis=0, keepdims=True)
            total = jnp.zeros((step, TILE), F32)
            for k in range(0, width, step):
                p = jnp.exp(logits[k:k + step, :] - peak)
                total = total + p
                p1, p2 = split(p)
                high[k:k + step, cols] = p1
                low[k:k + step, cols] = p2.astype(BF16)
            total = jnp.sum(total, axis=0, keepdims=True)
            for j in range(TILE // LANES):
                row = pl.ds(i * (TILE // LANES) + j, 1)
                peaks[row, :] = peak[:, j * LANES:(j + 1) * LANES]
                sums[row, :] = total[:, j * LANES:(j + 1) * LANES]
            return 0

        lax.fori_loop(0, cells // TILE, score, 0)

        norms[r, me_cent] = peaks[...] + jnp.log(sums[...])
        if r == 0:
            pl.semaphore_wait(barrier, n_cent + n_cells - 2)
        copies = []
        for d in range(1, n_cent):
            copy = pltpu.make_async_remote_copy(
                src_ref=norms.at[r, me_cent],
                dst_ref=norms.at[r, me_cent],
                send_sem=norm_send.at[r, d],
                recv_sem=norm_recv.at[r, d],
                device_id={"cent": lax.rem(me_cent + d, n_cent)},
                device_id_type=MESH,
            )
            copy.start()
            copies.append(copy)
        for copy in copies:
            copy.wait()
        top = norms[r, 0]
        for d in range(1, n_cent):
            top = jnp.maximum(top, norms[r, d])
        total = jnp.zeros((rows, LANES), F32)
        for d in range(n_cent):
            total = total + jnp.exp(norms[r, d] - top)
        norm = top + jnp.log(total)
        if r == ROUNDS - 1:
            norm_ref[...] = norm
        factor[...] = weight_ref[...] * jnp.exp(peaks[...] - norm)

        partial[...] = jnp.zeros_like(partial)

        def gather(i, _):
            cols = pl.ds(pl.multiple_of(i * TILE2, TILE2), TILE2)
            f = jnp.concatenate(
                [factor[pl.ds(i * (TILE2 // LANES) + j, 1), :] for j in range(TILE2 // LANES)], axis=1
            )
            g1, g2 = split(embed_ref[:, cols] * f)
            f1, f2 = split(jnp.broadcast_to(f, (features, TILE2)))
            scaled = jnp.concatenate([g1, g2.astype(BF16), f1, f2.astype(BF16)], axis=0)
            dims = (((1,), (1,)), ((), ()))
            partial[...] += lax.dot_general(
                high[:, cols], scaled, dims, preferred_element_type=F32
            ) + lax.dot_general(low[:, cols], scaled, dims, preferred_element_type=F32)
            return 0

        lax.fori_loop(0, cells // TILE2, gather, 0)

        moment = partial[:, :LANES]
        moment = moment + pltpu.roll(moment, features, 1)
        mass = partial[:, LANES:]
        mass = mass + pltpu.roll(mass, features, 1)
        partial[:, :LANES] = jnp.where(left, moment, mass)

        copies = []
        for d in range(1, n_cells):
            peer = lax.rem(me_cells + d, n_cells)
            copy = pltpu.make_async_remote_copy(
                src_ref=partial.at[pl.ds(pl.multiple_of(peer * chunk, chunk), chunk), pl.ds(0, LANES)],
                dst_ref=parts.at[r, d],
                send_sem=part_send.at[r, d],
                recv_sem=part_recv.at[r, d],
                device_id={"cells": peer},
                device_id_type=MESH,
            )
            copy.start()
            copies.append(copy)
        mine = pl.ds(pl.multiple_of(me_cells * chunk, chunk), chunk)
        total = partial[mine, pl.ds(0, LANES)]
        for copy in copies:
            copy.wait()
        for d in range(1, n_cells):
            total = total + parts[r, d]
        fresh = (total + PRIOR * current[r, mine, :]) / (pltpu.roll(total, features, 1) + PRIOR)
        current[r + 1, mine, :] = jnp.where(
            lax.broadcasted_iota(jnp.int32, (chunk, LANES), 1) < features,
            fresh,
            pltpu.roll(fresh, features, 1),
        )
        copies = []
        for d in range(1, n_cells):
            copy = pltpu.make_async_remote_copy(
                src_ref=current.at[r + 1, mine],
                dst_ref=current.at[r + 1, mine],
                send_sem=new_send.at[r, d],
                recv_sem=new_recv.at[r, d],
                device_id={"cells": lax.rem(me_cells + d, n_cells)},
                device_id_type=MESH,
            )
            copy.start()
            copies.append(copy)
        for copy in copies:
            copy.wait()

    out_ref[...] = current[ROUNDS].T[:features, :]


def on_device(embed, centroids, cell_weight):
    n_cells = lax.axis_size("cells")
    n_cent = lax.axis_size("cent")
    features, cells = embed.shape
    width = centroids.shape[1]
    rows = cells // LANES
    vmem = pl.BlockSpec(memory_space=pltpu.VMEM)
    dma = pltpu.SemaphoreType.DMA
    current, norms = pl.pallas_call(
        functools.partial(kernel, n_cells, n_cent),
        out_shape=(
            jax.ShapeDtypeStruct((features, width), F32),
            jax.ShapeDtypeStruct((rows, LANES), F32),
        ),
        in_specs=[vmem] * 3,
        out_specs=(vmem, vmem),
        scratch_shapes=[
            pltpu.VMEM((8 * features, cells), BF16),
            pltpu.VMEM((width, 4 * LANES), BF16),
            pltpu.VMEM((width, cells), BF16),
            pltpu.VMEM((width, cells), BF16),
            pltpu.VMEM((width, TILE), F32),
            pltpu.VMEM((rows, LANES), F32),
            pltpu.VMEM((rows, LANES), F32),
            pltpu.VMEM((rows, LANES), F32),
            pltpu.VMEM((ROUNDS + 1, width, LANES), F32),
            pltpu.VMEM((width, 2 * LANES), F32),
            pltpu.VMEM((ROUNDS, n_cent, rows, LANES), F32),
            pltpu.VMEM((ROUNDS, n_cells, width // n_cells, LANES), F32),
            dma((ROUNDS, n_cent)),
            dma((ROUNDS, n_cent)),
            dma((ROUNDS, n_cells)),
            dma((ROUNDS, n_cells)),
            dma((ROUNDS, n_cells)),
            dma((ROUNDS, n_cells)),
        ],
        compiler_params=pltpu.CompilerParams(
            collective_id=0, has_side_effects=True, vmem_limit_bytes=56 * 1024 * 1024
        ),
    )(embed, centroids, cell_weight.reshape(rows, LANES))
    return (current, norms.reshape(cells))


def solution(mesh):
    in_specs = (P(None, "cells"), P(None, "cent"), P("cells"))
    out_specs = (P(None, "cent"), P("cells"))
    return jax.shard_map(
        on_device, mesh=mesh, in_specs=in_specs, out_specs=out_specs, check_vma=False
    )
```

time: 350 us -> 64.4 us (0.18)
  waiting for transfers between devices: 174 us -> 0 us
  blocking collectives: 101 us -> 0 us
  Pallas kernels: 0 us -> 61.4 us
  matrix products: 37.2 us -> 0 us
  between operations: 14.2 us -> 0.65 us
  local copies, waits for them, and re-layouts: 11.4 us -> 2.18 us
  other arithmetic: 8.98 us -> 0 us
    psum x2 -> x0, waiting for transfers between devices: 174 us -> none  [on_device(): moment, masses = lax.psum((moment, masses), ('cells', 'cent'))]
    psum x2 -> x0, blocking collectives: 79.4 us -> none  [on_device(): moment, masses = lax.psum((moment, masses), ('cells', 'cent'))]
    pallas_call x0 -> x1, Pallas kernels: none -> 61.4 us  [on_device(): pl.pallas_call(functools.partial(kernel, n_cells, n_cent), out_shape=(jax...]
    dot_general x8 -> x0, matrix products: 37.2 us -> none  [the longest x4 22 us: add_shares(): jnp.dot(points, shares, precision=lax.Precision.HIGHEST)]
    all_gather x3 -> x0, blocking collectives: 21.4 us -> none  [the longest x2 16.2 us: on_device(): gathered = lax.all_gather(current, 'cent', axis=1, tiled=True)]
    reduce_sum x10 -> x0, other arithmetic: 6.23 us -> none  [the longest x4 3.31 us: add_shares(): masses = totals[1] + jnp.sum(shares, axis=0)]
    while x8 -> x0, local copies, waits for them, and re-layouts: 4.53 us -> none
  transfers between devices with their start and end apart: 2 -> 0, of which waited for: 2 -> 0; matrix products, arithmetic and copies ran while one was open for 0% -> 0% of each run, Pallas kernels for 0% -> 0%
where the time goes in v1:
time: 64.4 us; the launch traced here: 64.3 us
  Pallas kernels  61.4 us (95%)
  local copies, waits for them, and re-layouts  2.18 us (3%)
  between operations  0.65 us (1%)
    pallas_call x1, Pallas kernels, on_device(): pl.pallas_call(functools.partial(kernel, n_cells, n_cent), out_shape=(jax...  61.4 us
    unnamed x4, local copies, waits for them, and re-layouts  2.18 us

profile of v1, /device:TPU:0, one launch (start us, length us, event | category | flops | bytes accessed | tf_op | source)
XLA Modules:
  0.0 64.3 jit_solution(7415455531513969430)
XLA Ops:
  0.6 61.4 %shard_map.50 = (f32[64,512]{1,0:T(8,128)}, f32[32,128]{1,0:T(8,128)}) custom-call(f32[64,4096]{1,0:T(8,128)} %embed_ref.1, f32[64,512]{1,0:T(8,128)} %cent_ref.1, f32[32,128]{1,0:T(8,128)} %bitcast.2), custom_call_target="tpu_custom_call" | custom-call | tf_op jit(solution)/shard_map/pallas_call | solution.py:212
  62.1 0.0 copy-start
  62.1 1.6 %copy.7 = f32[64,512]{1,0:T(8,128)} copy(f32[64,512]{1,0:T(8,128)} %get-tuple-element.8) | data formatting | bytes 262144
  63.6 0.0 copy-done
  63.6 0.6 copy.8
Async XLA Ops:
  62.1 1.6 %copy-start = (f32[32,128]{1,0:T(8,128)S(1)}, f32[32,128]{1,0:T(8,128)}, u32[]{:S(2)}) copy-start(f32[32,128]{1,0:T(8,128)} %get-tuple-element.5) | copy-start | bytes 49156

commit v2 on v1

--- a/solution.py
+++ b/solution.py
@@ -12,6 +12,7 @@
 PRIOR = 1.0
 TILE = 256
 TILE2 = 1024
+HALVES = 2
 LANES = 128
 MESH = pl.DeviceIdType.MESH
 BF16 = jnp.bfloat16
@@ -28,13 +29,16 @@
     embed_ref, cent_ref, weight_ref,
     out_ref, norm_ref,
     points, table, high, low, logits, peaks, sums, factor,
-    current, partial, norms, parts,
+    packed, partial, outgoing, norms, parts,
     norm_send, norm_recv, part_send, part_recv, new_send, new_recv,
 ):
     features, cells = embed_ref.shape
     width = cent_ref.shape[1]
     rows = cells // LANES
     chunk = width // n_cells
+    half = rows // HALVES
+    tiles = cells // TILE // HALVES
+    tiles2 = cells // TILE2 // HALVES
     me_cells = lax.axis_index("cells")
     me_cent = lax.axis_index("cent")
 
@@ -61,12 +65,26 @@
     lax.fori_loop(0, cells // TILE, stack_points, 0)
 
     lane = lax.broadcasted_iota(jnp.int32, (width, LANES), 1)
+    row = lax.broadcasted_iota(jnp.int32, (width, LANES), 0)
     left = lane < features
+    pair = chunk // 2
+    left_pair = lax.broadcasted_iota(jnp.int32, (n_cells, pair, LANES), 2) < features
+
+    def pack(x):
+        x = x.reshape(n_cells, 2, pair, LANES)
+        return jnp.where(left_pair, x[:, 0], x[:, 1])
+
+    def unpack(x):
+        other = pltpu.roll(x, features, 2)
+        low_rows = jnp.where(left_pair, x, other)
+        high_rows = jnp.where(left_pair, other, x)
+        return jnp.stack([low_rows, high_rows], axis=1).reshape(width, LANES)
+
     start = cent_ref[...].T
-    current[0] = jnp.concatenate([start, start], axis=1)
+    both = jnp.concatenate([start, start], axis=1)
+    packed[0] = pack(both)
 
     for r in range(ROUNDS):
-        both = current[r]
         half_square = 0.5 * jnp.sum(jnp.where(left, both * both, 0.0), axis=1, keepdims=True)
         c1, rest = split(both * INV_TEMP)
         c2, rest = split(rest)
@@ -104,35 +122,26 @@
                 sums[row, :] = total[:, j * LANES:(j + 1) * LANES]
             return 0
 
-        lax.fori_loop(0, cells // TILE, score, 0)
-
-        norms[r, me_cent] = peaks[...] + jnp.log(sums[...])
-        if r == 0:
-            pl.semaphore_wait(barrier, n_cent + n_cells - 2)
-        copies = []
-        for d in range(1, n_cent):
-            copy = pltpu.make_async_remote_copy(
-                src_ref=norms.at[r, me_cent],
-                dst_ref=norms.at[r, me_cent],
-                send_sem=norm_send.at[r, d],
-                recv_sem=norm_recv.at[r, d],
-                device_id={"cent": lax.rem(me_cent + d, n_cent)},
-                device_id_type=MESH,
-            )
-            copy.start()
-            copies.append(copy)
-        for copy in copies:
-            copy.wait()
-        top = norms[r, 0]
-        for d in range(1, n_cent):
-            top = jnp.maximum(top, norms[r, d])
-        total = jnp.zeros((rows, LANES), F32)
-        for d in range(n_cent):
-            total = total + jnp.exp(norms[r, d] - top)
-        norm = top + jnp.log(total)
-        if r == ROUNDS - 1:
-            norm_ref[...] = norm
-        factor[...] = weight_ref[...] * jnp.exp(peaks[...] - norm)
+        pending = []
+        for h in range(HALVES):
+            lax.fori_loop(h * tiles, (h + 1) * tiles, score, 0)
+            span = pl.ds(h * half, half)
+            norms[r, me_cent, span] = peaks[span] + jnp.log(sums[span])
+            if r == 0 and h == 0:
+                pl.semaphore_wait(barrier, n_cent + n_cells - 2)
+            copies = []
+            for d in range(1, n_cent):
+                copy = pltpu.make_async_remote_copy(
+                    src_ref=norms.at[r, me_cent, span],
+                    dst_ref=norms.at[r, me_cent, span],
+                    send_sem=norm_send.at[r, h, d],
+                    recv_sem=norm_recv.at[r, h, d],
+                    device_id={"cent": lax.rem(me_cent + d, n_cent)},
+                    device_id_type=MESH,
+                )
+                copy.start()
+                copies.append(copy)
+            pending.append(copies)
 
         partial[...] = jnp.zeros_like(partial)
 
@@ -150,19 +159,36 @@
             ) + lax.dot_general(low[:, cols], scaled, dims, preferred_element_type=F32)
             return 0
 
-        lax.fori_loop(0, cells // TILE2, gather, 0)
+        for h in range(HALVES):
+            for copy in pending[h]:
+                copy.wait()
+            span = pl.ds(h * half, half)
+            top = norms[r, 0, span]
+            for d in range(1, n_cent):
+                top = jnp.maximum(top, norms[r, d, span])
+            total = jnp.zeros((half, LANES), F32)
+            for d in range(n_cent):
+                total = total + jnp.exp(norms[r, d, span] - top)
+            norm = top + jnp.log(total)
+            if r == ROUNDS - 1:
+                norm_ref[span] = norm
+            factor[span] = weight_ref[span] * jnp.exp(peaks[span] - norm)
+            lax.fori_loop(h * tiles2, (h + 1) * tiles2, gather, 0)
 
         moment = partial[:, :LANES]
         moment = moment + pltpu.roll(moment, features, 1)
         mass = partial[:, LANES:]
         mass = mass + pltpu.roll(mass, features, 1)
-        partial[:, :LANES] = jnp.where(left, moment, mass)
+        outgoing[:, :pair] = pack(moment)
+        mass = jnp.where(lane == lax.rem(row, chunk), mass, 0.0)
+        mass = jnp.sum(mass.reshape(n_cells, chunk, LANES), axis=1, keepdims=True)
+        outgoing[:, pair:] = jnp.broadcast_to(mass, (n_cells, 8, LANES))
 
         copies = []
         for d in range(1, n_cells):
             peer = lax.rem(me_cells + d, n_cells)
             copy = pltpu.make_async_remote_copy(
-                src_ref=partial.at[pl.ds(pl.multiple_of(peer * chunk, chunk), chunk), pl.ds(0, LANES)],
+                src_ref=outgoing.at[peer],
                 dst_ref=parts.at[r, d],
                 send_sem=part_send.at[r, d],
                 recv_sem=part_recv.at[r, d],
@@ -171,23 +197,22 @@
             )
             copy.start()
             copies.append(copy)
-        mine = pl.ds(pl.multiple_of(me_cells * chunk, chunk), chunk)
-        total = partial[mine, pl.ds(0, LANES)]
-        for copy in copies:
-            copy.wait()
+        total = outgoing[me_cells]
         for d in range(1, n_cells):
+            copies[d - 1].wait()
             total = total + parts[r, d]
-        fresh = (total + PRIOR * current[r, mine, :]) / (pltpu.roll(total, features, 1) + PRIOR)
-        current[r + 1, mine, :] = jnp.where(
-            lax.broadcasted_iota(jnp.int32, (chunk, LANES), 1) < features,
-            fresh,
-            pltpu.roll(fresh, features, 1),
-        )
+        mass = jnp.broadcast_to(total[pair:pair + 1], (pair, LANES))
+        lane_p = lax.broadcasted_iota(jnp.int32, (pair, LANES), 1)
+        row_p = lax.broadcasted_iota(jnp.int32, (pair, LANES), 0)
+        mass_l = jnp.sum(jnp.where(lane_p == row_p, mass, 0.0), axis=1, keepdims=True)
+        mass_r = jnp.sum(jnp.where(lane_p == row_p + pair, mass, 0.0), axis=1, keepdims=True)
+        mass = jnp.where(lane_p < features, mass_l, mass_r)
+        packed[r + 1, me_cells] = (total[:pair] + PRIOR * packed[r, me_cells]) / (mass + PRIOR)
         copies = []
         for d in range(1, n_cells):
             copy = pltpu.make_async_remote_copy(
-                src_ref=current.at[r + 1, mine],
-                dst_ref=current.at[r + 1, mine],
+                src_ref=packed.at[r + 1, me_cells],
+                dst_ref=packed.at[r + 1, me_cells],
                 send_sem=new_send.at[r, d],
                 recv_sem=new_recv.at[r, d],
                 device_id={"cells": lax.rem(me_cells + d, n_cells)},
@@ -197,8 +222,9 @@
             copies.append(copy)
         for copy in copies:
             copy.wait()
-
-    out_ref[...] = current[ROUNDS].T[:features, :]
+        both = unpack(packed[r + 1])
+
+    out_ref[...] = both.T[:features, :]
 
 
 def on_device(embed, centroids, cell_weight):
@@ -207,6 +233,7 @@
     features, cells = embed.shape
     width = centroids.shape[1]
     rows = cells // LANES
+    pair = width // n_cells // 2
     vmem = pl.BlockSpec(memory_space=pltpu.VMEM)
     dma = pltpu.SemaphoreType.DMA
     current, norms = pl.pallas_call(
@@ -226,12 +253,13 @@
             pltpu.VMEM((rows, LANES), F32),
             pltpu.VMEM((rows, LANES), F32),
             pltpu.VMEM((rows, LANES), F32),
-            pltpu.VMEM((ROUNDS + 1, width, LANES), F32),
+            pltpu.VMEM((ROUNDS + 1, n_cells, pair, LANES), F32),
             pltpu.VMEM((width, 2 * LANES), F32),
+            pltpu.VMEM((n_cells, pair + 8, LANES), F32),
             pltpu.VMEM((ROUNDS, n_cent, rows, LANES), F32),
-            pltpu.VMEM((ROUNDS, n_cells, width // n_cells, LANES), F32),
-            dma((ROUNDS, n_cent)),
-            dma((ROUNDS, n_cent)),
+            pltpu.VMEM((ROUNDS, n_cells, pair + 8, LANES), F32),
+            dma((ROUNDS, HALVES, n_cent)),
+            dma((ROUNDS, HALVES, n_cent)),
             dma((ROUNDS, n_cells)),
             dma((ROUNDS, n_cells)),
             dma((ROUNDS, n_cells)),

time: 64.4 us -> 54.7 us (0.85)
  Pallas kernels: 61.4 us -> 51.7 us
    pallas_call x1, Pallas kernels: 61.4 us -> 51.7 us  [on_device(): pl.pallas_call(functools.partial(kernel, n_cells, n_cent), out_shape=(jax...]
where the time goes in v2:
time: 54.7 us; the launch traced here: 54.6 us
  Pallas kernels  51.7 us (95%)
  local copies, waits for them, and re-layouts  2.18 us (4%)
  between operations  0.65 us (1%)
    pallas_call x1, Pallas kernels, on_device(): pl.pallas_call(functools.partial(kernel, n_cells, n_cent), out_shape=(jax...  51.7 us
    unnamed x4, local copies, waits for them, and re-layouts  2.18 us

profile of v2, /device:TPU:0, one launch (start us, length us, event | category | flops | bytes accessed | tf_op | source)
XLA Modules:
  0.0 54.6 jit_solution(14043565933346369240)
XLA Ops:
  0.6 51.7 %shard_map.50 = (f32[64,512]{1,0:T(8,128)}, f32[32,128]{1,0:T(8,128)}) custom-call(f32[64,4096]{1,0:T(8,128)} %embed_ref.1, f32[64,512]{1,0:T(8,128)} %cent_ref.1, f32[32,128]{1,0:T(8,128)} %bitcast.2), custom_call_target="tpu_custom_call" | custom-call | tf_op jit(solution)/shard_map/pallas_call | solution.py:239
  52.4 0.0 copy-start
  52.4 1.6 %copy.7 = f32[64,512]{1,0:T(8,128)} copy(f32[64,512]{1,0:T(8,128)} %get-tuple-element.8) | data formatting | bytes 262144
  53.9 0.0 copy-done
  54.0 0.6 %copy.8 = f32[4096]{0:T(1024)} copy(f32[4096]{0:T(1024)S(1)} %bitcast.3) | data formatting | bytes 32768
Async XLA Ops:
  52.4 1.6 %copy-start = (f32[32,128]{1,0:T(8,128)S(1)}, f32[32,128]{1,0:T(8,128)}, u32[]{:S(2)}) copy-start(f32[32,128]{1,0:T(8,128)} %get-tuple-element.5) | copy-start | bytes 49156

commit v3 on v1

v3 whole, which is shorter than its diff:
```python
import functools

import jax
import jax.numpy as jnp
from jax import lax
from jax.experimental import pallas as pl
from jax.experimental.pallas import tpu as pltpu
from jax.sharding import PartitionSpec as P

ROUNDS = 2
INV_TEMP = 0.125
PRIOR = 1.0
TILE = 256
HALVES = 2
LANES = 128
MESH = pl.DeviceIdType.MESH
BF16 = jnp.bfloat16
F32 = jnp.float32


def split(x):
    high = x.astype(BF16)
    return high, x - high.astype(F32)


def kernel(
    n_cells, n_cent, blocks,
    embed_ref, cent_ref, weight_ref,
    out_ref, norm_ref,
    points, table, high, low, logits_a, logits_b, peaks, sums, factor,
    packed, partial, outgoing, norms, parts,
    norm_send, norm_recv, part_send, part_recv, new_send, new_recv,
):
    features, cells = embed_ref.shape
    width = cent_ref.shape[1] // blocks
    rows = cells // LANES
    chunk = width // n_cells
    pair = chunk // 2
    half = rows // HALVES
    half_cells = cells // HALVES
    tiles = cells // TILE // HALVES
    me_cells = lax.axis_index("cells")
    me_cent = lax.axis_index("cent")

    barrier = pltpu.get_barrier_semaphore()
    for d in range(1, n_cent):
        pl.semaphore_signal(
            barrier, inc=1, device_id={"cent": lax.rem(me_cent + d, n_cent)}, device_id_type=MESH
        )
    for d in range(1, n_cells):
        pl.semaphore_signal(
            barrier, inc=1, device_id={"cells": lax.rem(me_cells + d, n_cells)}, device_id_type=MESH
        )

    def stack_points(i, _):
        cols = pl.ds(pl.multiple_of(i * TILE, TILE), TILE)
        e1, rest = split(embed_ref[:, cols])
        e2, rest = split(rest)
        e3 = rest.astype(BF16)
        for j, term in enumerate((e1, e1, e2, e2, e1, e3)):
            points[j * features:(j + 1) * features, cols] = term
        points[6 * features:, cols] = jnp.ones((2 * features, TILE), BF16)
        return 0

    lax.fori_loop(0, cells // TILE, stack_points, 0)

    lane = lax.broadcasted_iota(jnp.int32, (width, LANES), 1)
    row = lax.broadcasted_iota(jnp.int32, (width, LANES), 0)
    left = lane < features
    left_pair = lax.broadcasted_iota(jnp.int32, (n_cells, pair, LANES), 2) < features

    def pack(x):
        x = x.reshape(n_cells, 2, pair, LANES)
        return jnp.where(left_pair, x[:, 0], x[:, 1])

    def unpack(x):
        other = pltpu.roll(x, features, 2)
        low_rows = jnp.where(left_pair, x, other)
        high_rows = jnp.where(left_pair, other, x)
        return jnp.stack([low_rows, high_rows], axis=1).reshape(width, LANES)

    def load_block(r, b):
        if r == 0:
            start = cent_ref[:, b * width:(b + 1) * width].T
            both = jnp.concatenate([start, start], axis=1)
            packed[0, b] = pack(both)
            return both
        for copy in arriving[b]:
            copy.wait()
        return unpack(packed[r, b])

    def fill_table(b, both):
        out = slice(b * width, (b + 1) * width)
        half_square = 0.5 * jnp.sum(jnp.where(left, both * both, 0.0), axis=1, keepdims=True)
        c1, rest = split(both * INV_TEMP)
        c2, rest = split(rest)
        c3 = rest
        h1, rest = split(jnp.broadcast_to(half_square * -INV_TEMP, (width, LANES)))
        h2, h3 = split(rest)
        c1, c2, h1, h2 = (x.astype(F32) for x in (c1, c2, h1, h2))
        first = jnp.where(left, c1, c2).astype(BF16)
        table[out, 0:LANES] = first
        table[out, LANES:2 * LANES] = first
        table[out, 2 * LANES:3 * LANES] = jnp.where(left, c3, c1).astype(BF16)
        table[out, 3 * LANES:] = jnp.where(
            lane == 0, h1, jnp.where(lane == 1, h2, jnp.where(lane == 2, h3, 0.0))
        ).astype(BF16)

    def score(b, h):
        base = b * width

        def columns(i):
            return pl.ds(pl.multiple_of(i * TILE, TILE), TILE)

        def product(buffer, i):
            buffer[...] = jnp.dot(
                table[base:base + width, :], points[:, columns(i)], preferred_element_type=F32
            )

        def weigh(buffer, i):
            cols = columns(i)
            step = 64
            peak = buffer[0:step, :]
            for k in range(step, width, step):
                peak = jnp.maximum(peak, buffer[k:k + step, :])
            peak = jnp.max(peak, axis=0, keepdims=True)
            total = jnp.zeros((step, TILE), F32)
            for k in range(0, width, step):
                p = jnp.exp(buffer[k:k + step, :] - peak)
                total = total + p
                p1, p2 = split(p)
                high[base + k:base + k + step, cols] = p1
                low[base + k:base + k + step, cols] = p2.astype(BF16)
            total = jnp.sum(total, axis=0, keepdims=True)
            for j in range(TILE // LANES):
                at = pl.ds(i * (TILE // LANES) + j, 1)
                peaks[b, at, :] = peak[:, j * LANES:(j + 1) * LANES]
                sums[b, at, :] = total[:, j * LANES:(j + 1) * LANES]

        first = h * tiles

        def step_pair(i, _):
            at = first + 2 * i
            product(logits_b, at + 1)
            weigh(logits_a, at)
            product(logits_a, at + 2)
            weigh(logits_b, at + 1)
            return 0

        product(logits_a, first)
        lax.fori_loop(0, tiles // 2 - 1, step_pair, 0)
        product(logits_b, first + tiles - 1)
        weigh(logits_a, first + tiles - 2)
        weigh(logits_b, first + tiles - 1)

    def send_norms(r, h):
        span = pl.ds(h * half, half)
        top = peaks[0, span]
        for b in range(1, blocks):
            top = jnp.maximum(top, peaks[b, span])
        total = jnp.zeros((half, LANES), F32)
        for b in range(blocks):
            total = total + sums[b, span] * jnp.exp(peaks[b, span] - top)
        norms[r, me_cent, span] = top + jnp.log(total)
        if r == 0 and h == 0:
            pl.semaphore_wait(barrier, n_cent + n_cells - 2)
        copies = []
        for d in range(1, n_cent):
            copy = pltpu.make_async_remote_copy(
                src_ref=norms.at[r, me_cent, span],
                dst_ref=norms.at[r, me_cent, span],
                send_sem=norm_send.at[r, h, d],
                recv_sem=norm_recv.at[r, h, d],
                device_id={"cent": lax.rem(me_cent + d, n_cent)},
                device_id_type=MESH,
            )
            copy.start()
            copies.append(copy)
        return copies

    def take_norms(r, h, copies):
        for copy in copies:
            copy.wait()
        span = pl.ds(h * half, half)
        top = norms[r, 0, span]
        for d in range(1, n_cent):
            top = jnp.maximum(top, norms[r, d, span])
        total = jnp.zeros((half, LANES), F32)
        for d in range(n_cent):
            total = total + jnp.exp(norms[r, d, span] - top)
        norm = top + jnp.log(total)
        if r == ROUNDS - 1:
            norm_ref[span] = norm
        for b in range(blocks):
            factor[b, span] = weight_ref[span] * jnp.exp(peaks[b, span] - norm)

    def gather(b, h):
        cols = pl.ds(h * half_cells, half_cells)
        out = slice(b * width, (b + 1) * width)
        f = jnp.concatenate([factor[b, h * half + j:h * half + j + 1, :] for j in range(half)], axis=1)
        g1, g2 = split(embed_ref[:, cols] * f)
        f1, f2 = split(jnp.broadcast_to(f, (features, half_cells)))
        scaled = jnp.concatenate([g1, g2.astype(BF16), f1, f2.astype(BF16)], axis=0)
        dims = (((1,), (1,)), ((), ()))
        sums_now = lax.dot_general(
            high[out, cols], scaled, dims, preferred_element_type=F32
        ) + lax.dot_general(low[out, cols], scaled, dims, preferred_element_type=F32)
        if h == 0:
            partial[...] = sums_now
        else:
            partial[...] += sums_now

    def send_parts(r, b):
        moment = partial[:, :LANES]
        moment = moment + pltpu.roll(moment, features, 1)
        mass = partial[:, LANES:]
        mass = mass + pltpu.roll(mass, features, 1)
        outgoing[r, b, :, :pair] = pack(moment)
        mass = jnp.where(lane == lax.rem(row, chunk), mass, 0.0)
        mass = jnp.sum(mass.reshape(n_cells, chunk, LANES), axis=1, keepdims=True)
        outgoing[r, b, :, pair:] = jnp.broadcast_to(mass, (n_cells, 8, LANES))
        copies = []
        for d in range(1, n_cells):
            peer = lax.rem(me_cells + d, n_cells)
            copy = pltpu.make_async_remote_copy(
                src_ref=outgoing.at[r, b, peer],
                dst_ref=parts.at[r, b, d],
                send_sem=part_send.at[r, b, d],
                recv_sem=part_recv.at[r, b, d],
                device_id={"cells": peer},
                device_id_type=MESH,
            )
            copy.start()
            copies.append(copy)
        return copies

    def send_new(r, b, copies):
        total = outgoing[r, b, me_cells]
        for d in range(1, n_cells):
            copies[d - 1].wait()
            total = total + parts[r, b, d]
        mass = jnp.broadcast_to(total[pair:pair + 1], (pair, LANES))
        lane_p = lax.broadcasted_iota(jnp.int32, (pair, LANES), 1)
        row_p = lax.broadcasted_iota(jnp.int32, (pair, LANES), 0)
        mass_l = jnp.sum(jnp.where(lane_p == row_p, mass, 0.0), axis=1, keepdims=True)
        mass_r = jnp.sum(jnp.where(lane_p == row_p + pair, mass, 0.0), axis=1, keepdims=True)
        mass = jnp.where(lane_p < features, mass_l, mass_r)
        packed[r + 1, b, me_cells] = (total[:pair] + PRIOR * packed[r, b, me_cells]) / (mass + PRIOR)
        copies = []
        for d in range(1, n_cells):
            copy = pltpu.make_async_remote_copy(
                src_ref=packed.at[r + 1, b, me_cells],
                dst_ref=packed.at[r + 1, b, me_cells],
                send_sem=new_send.at[r, b, d],
                recv_sem=new_recv.at[r, b, d],
                device_id={"cells": lax.rem(me_cells + d, n_cells)},
                device_id_type=MESH,
            )
            copy.start()
            copies.append(copy)
        return copies

    arriving = []
    for r in range(ROUNDS):
        pending = []
        for b in range(blocks):
            fill_table(b, load_block(r, b))
            for h in range(HALVES):
                score(b, h)
                if b == blocks - 1:
                    pending.append(send_norms(r, h))
        leaving = []
        for b in range(blocks):
            for h in range(HALVES):
                if b == 0:
                    take_norms(r, h, pending[h])
                gather(b, h)
            leaving.append(send_parts(r, b))
        arriving = [send_new(r, b, leaving[b]) for b in range(blocks)]
    for b in range(blocks):
        both = load_block(ROUNDS, b)
        out_ref[:, b * width:(b + 1) * width] = both.T[:features, :]


def hand_over(current_ref, norm_ref, out_ref, norm_out_ref):
    out_ref[...] = current_ref[...]
    norm_out_ref[...] = norm_ref[...]


def on_device(embed, centroids, cell_weight):
    n_cells = lax.axis_size("cells")
    n_cent = lax.axis_size("cent")
    features, cells = embed.shape
    width = centroids.shape[1]
    rows = cells // LANES
    blocks = 1
    block = width // blocks
    pair = block // n_cells // 2
    vmem = pl.BlockSpec(memory_space=pltpu.VMEM)
    dma = pltpu.SemaphoreType.DMA
    current, norms = pl.pallas_call(
        functools.partial(kernel, n_cells, n_cent, blocks),
        out_shape=(
            jax.ShapeDtypeStruct((features, width), F32),
            jax.ShapeDtypeStruct((rows, LANES), F32),
        ),
        in_specs=[vmem] * 3,
        out_specs=(vmem, vmem),
        scratch_shapes=[
            pltpu.VMEM((8 * features, cells), BF16),
            pltpu.VMEM((width, 4 * LANES), BF16),
            pltpu.VMEM((width, cells), BF16),
            pltpu.VMEM((width, cells), BF16),
            pltpu.VMEM((block, TILE), F32),
            pltpu.VMEM((block, TILE), F32),
            pltpu.VMEM((blocks, rows, LANES), F32),
            pltpu.VMEM((blocks, rows, LANES), F32),
            pltpu.VMEM((blocks, rows, LANES), F32),
            pltpu.VMEM((ROUNDS + 1, blocks, n_cells, pair, LANES), F32),
            pltpu.VMEM((block, 2 * LANES), F32),
            pltpu.VMEM((ROUNDS, blocks, n_cells, pair + 8, LANES), F32),
            pltpu.VMEM((ROUNDS, n_cent, rows, LANES), F32),
            pltpu.VMEM((ROUNDS, blocks, n_cells, pair + 8, LANES), F32),
            dma((ROUNDS, HALVES, n_cent)),
            dma((ROUNDS, HALVES, n_cent)),
            dma((ROUNDS, blocks, n_cells)),
            dma((ROUNDS, blocks, n_cells)),
            dma((ROUNDS, blocks, n_cells)),
            dma((ROUNDS, blocks, n_cells)),
        ],
        compiler_params=pltpu.CompilerParams(
            collective_id=0, has_side_effects=True, vmem_limit_bytes=56 * 1024 * 1024
        ),
    )(embed, centroids, cell_weight.reshape(rows, LANES))
    current, norms = pl.pallas_call(
        hand_over,
        out_shape=(
            jax.ShapeDtypeStruct((features, width), F32),
            jax.ShapeDtypeStruct((rows, LANES), F32),
        ),
        in_specs=[vmem] * 2,
        out_specs=(vmem, vmem),
    )(current, norms)
    return (current, norms.reshape(cells))


def solution(mesh):
    in_specs = (P(None, "cells"), P(None, "cent"), P("cells"))
    out_specs = (P(None, "cent"), P("cells"))
    return jax.shard_map(
        on_device, mesh=mesh, in_specs=in_specs, out_specs=out_specs, check_vma=False
    )
```

time: 64.4 us -> 54.1 us (0.84)
  Pallas kernels: 61.4 us -> 53.3 us
  local copies, waits for them, and re-layouts: 2.18 us -> 0 us
    pallas_call x1 -> x2, Pallas kernels: 61.4 us -> 53.3 us  [the longest x1 51.8 us: on_device(): pl.pallas_call(functools.partial(kernel, n_cells, n_cent, blocks), out_sh...]
    unnamed x4 -> x0, local copies, waits for them, and re-layouts: 2.18 us -> none
where the time goes in v3:
time: 54.1 us; the launch traced here: 54 us
  Pallas kernels  53.3 us (99%)
  between operations  0.64 us (1%)
    pallas_call x1, Pallas kernels, on_device(): pl.pallas_call(functools.partial(kernel, n_cells, n_cent, blocks), out_sh...  51.8 us
    pallas_call x1, Pallas kernels, on_device(): pl.pallas_call(hand_over, out_shape=(jax.ShapeDtypeStruct((features, widt...  1.57 us

profile of v3, /device:TPU:0, one launch (start us, length us, event | category | flops | bytes accessed | tf_op | source)
XLA Modules:
  0.0 54.0 jit_solution(5085595329922588092)
XLA Ops:
  0.6 51.8 %shard_map.50 = (f32[64,512]{1,0:T(8,128)}, f32[32,128]{1,0:T(8,128)}) custom-call(f32[64,4096]{1,0:T(8,128)} %embed_ref.1, f32[64,512]{1,0:T(8,128)} %cent_ref.1, f32[32,128]{1,0:T(8,128)} %bitcast.2), custom_call_target="tpu_custom_call" | custom-call | tf_op jit(solution)/shard_map/pallas_call | solution.py:301
  52.4 1.6 %shard_map.51 = (f32[64,512]{1,0:T(8,128)}, f32[32,128]{1,0:T(8,128)}) custom-call(f32[64,512]{1,0:T(8,128)} %get-tuple-element.6.current_ref, f32[32,128]{1,0:T(8,128)} %get-tuple-element.7.norm_ref), custom_call_target="tpu_custom_call" | custom-call | tf_op jit(solution)/shard_map/pallas_call | solution.py:335
